TPU v7x, 512 devices: a whole 4x4x16 slice. The times are simulated.
512 devices in a mesh: ctx: 16 (over z_lo, core), head: 32 (over z_hi, y, x).
Axes of the slice: x: 4, y: 4, z: 16 (z_hi: 2, z_lo: 8; z = z_hi * 8 + z_lo), core: 2. Of those that a mesh axis runs over, the one named last changes fastest.
Arguments:
- tokens: bfloat16 [4096, 4096], P('ctx', 'head'), may hold values from -6 to 6
- qkv_weight: bfloat16 [4096, 3, 4096], P(None, None, 'head'), may hold values from -0.09375 to 0.09375
- out_weight: bfloat16 [4096, 4096], P('head'), may hold values from -1 to 1
- signs: int32 [32, 2, 128], P('head'), may hold values from 0 to 1
- rows: int32 [32, 2, 64], P('head'), may hold values from 0 to 127
Outputs:
- mixed: bfloat16 [4096, 4096], P('ctx', 'head')
Inputs may be any that keep to these rules, and one draw needn't show every extreme that they name: `signs`: each sign bit s gives the sign 2 s - 1. `rows`: rows are drawn with repetition.
All inputs are finite; a program needn't handle non-finite values.
Results may differ from a plain program's by a relative error of at most 0.025.
Values may be sent and summed in bfloat16 or wider, within the bound.
A program may use at most 128 MiB of HBM per device.

v0:
```python
import math
import jax
import jax.numpy as jnp
from jax import lax
from jax.sharding import PartitionSpec as P

BLOCK = 256
score_scale = 2.0


def prefix(value, axis, join, neutral):
    place = lax.axis_index(axis)
    gathered = jax.tree.map(
        lambda a, kind: lax.all_gather(a.astype(kind), axis), value, (jnp.bfloat16, jnp.bfloat16)
    )
    state = jax.tree.map(lambda a, e: jnp.zeros_like(a) + jnp.asarray(e, a.dtype), value, neutral)

    def one(hop, state):
        return join(
            state,
            jax.tree.map(
                lambda a, own: lax.dynamic_index_in_dim(a, hop, 0, False).astype(own.dtype),
                gathered,
                value,
            ),
        )

    return lax.fori_loop(0, place, one, state)


def hadamard_table(size_hd):
    row_index = jnp.arange(size_hd, dtype=jnp.int32)[:, None]
    col_index = jnp.arange(size_hd, dtype=jnp.int32)[None, :]
    common = jnp.bitwise_and(row_index, col_index)
    parity = jnp.zeros((size_hd, size_hd), jnp.int32)
    for bit_place in range(size_hd.bit_length() - 1):
        parity = parity + jnp.bitwise_and(jnp.right_shift(common, bit_place), 1)
    return 1.0 - 2.0 * jnp.bitwise_and(parity, 1).astype(jnp.float32)


def sketch_matrix(signs, rows):
    size_hd = signs.shape[-1]
    hadamard = hadamard_table(size_hd)
    selector = (jnp.arange(size_hd, dtype=jnp.int32)[:, None] == rows[..., None, :]).astype(
        jnp.float32
    )
    columns = jnp.einsum("de,kief->kidf", hadamard, selector, precision=lax.Precision.HIGHEST)
    signed = (2 * signs - 1).astype(jnp.float32)
    return (signed[..., None] * columns).astype(jnp.bfloat16)


def normalize(raw_rows):
    scale_rows = lax.rsqrt(jnp.mean(raw_rows * raw_rows, axis=-1, keepdims=True) + 1e-06)
    return (raw_rows * scale_rows).astype(jnp.bfloat16)


def features(normed, sketch):
    size_hd = sketch.shape[2]
    size_m = sketch.shape[3]
    branches = jnp.einsum("tkd,kidm->tkim", normed, sketch, preferred_element_type=jnp.float32)
    factor = score_scale * score_scale / (size_hd * math.sqrt(size_m))
    sketched = factor * branches[:, :, 0, :] * branches[:, :, 1, :]
    squared = sketched[:, :, :, None] * sketched[:, :, None, :]
    return squared.reshape(sketched.shape[0], sketched.shape[1], size_m * size_m).astype(
        jnp.bfloat16
    )


def add_pair(earlier, later):
    return (earlier[0] + later[0], earlier[1] + later[1])


def shards(tokens, qkv_weight, out_weight, signs, rows):
    length = tokens.shape[0]
    local_heads = signs.shape[0]
    size_hd = signs.shape[2]
    model_width = qkv_weight.shape[0]
    flat_weight = qkv_weight.reshape(model_width, 3 * local_heads * size_hd)
    projected = jnp.dot(
        lax.all_gather(tokens, "head", axis=1, tiled=True),
        flat_weight,
        preferred_element_type=jnp.float32,
    )
    projected = projected.reshape(length, 3, local_heads, size_hd)
    normed_queries = normalize(projected[:, 0])
    normed_keys = normalize(projected[:, 1])
    values = projected[:, 2].astype(jnp.bfloat16)
    sketch = sketch_matrix(signs, rows)
    query_feats = features(normed_queries, sketch)
    key_feats = features(normed_keys, sketch)
    feat_width = query_feats.shape[2]
    nblocks = length // BLOCK
    qf = query_feats.reshape(nblocks, BLOCK, local_heads, feat_width)
    kf = key_feats.reshape(nblocks, BLOCK, local_heads, feat_width)
    vbk = values.reshape(nblocks, BLOCK, local_heads, size_hd)
    block_states = jnp.einsum("btkf,btkd->bkfd", kf, vbk, preferred_element_type=jnp.float32)
    block_sums = jnp.sum(kf, axis=1, dtype=jnp.float32)
    state_zero = jnp.zeros((local_heads, feat_width, size_hd), jnp.float32)
    sum_zero = jnp.zeros((local_heads, feat_width), jnp.float32)
    local_state = jnp.sum(block_states, axis=0)
    local_sum = jnp.sum(block_sums, axis=0)
    earlier_state, earlier_sum = prefix(
        (local_state, local_sum), "ctx", add_pair, (state_zero, sum_zero)
    )
    inner_state = jnp.concatenate([state_zero[None], jnp.cumsum(block_states, axis=0)[:-1]], axis=0)
    inner_sum = jnp.concatenate([sum_zero[None], jnp.cumsum(block_sums, axis=0)[:-1]], axis=0)
    prefix_state = (earlier_state[None] + inner_state).astype(jnp.bfloat16)
    prefix_sum = (earlier_sum[None] + inner_sum).astype(jnp.bfloat16)
    num_state = jnp.einsum("btkf,bkfd->btkd", qf, prefix_state, preferred_element_type=jnp.float32)
    den_state = jnp.einsum("btkf,bkf->btk", qf, prefix_sum, preferred_element_type=jnp.float32)
    qblk = normed_queries.reshape(nblocks, BLOCK, local_heads, size_hd)
    kblk = normed_keys.reshape(nblocks, BLOCK, local_heads, size_hd)
    scores = jnp.einsum("btkd,bpkd->bktp", qblk, kblk, preferred_element_type=jnp.float32)
    causal = (
        jnp.arange(BLOCK, dtype=jnp.int32)[:, None] >= jnp.arange(BLOCK, dtype=jnp.int32)[None, :]
    ).astype(jnp.float32)
    weights = (score_scale * scores / size_hd) ** 4 * causal[None, None]
    den_diag = jnp.sum(weights, axis=-1).transpose(0, 2, 1)
    weights_b = weights.astype(jnp.bfloat16)
    num_diag = jnp.einsum("bktp,bpkd->btkd", weights_b, vbk, preferred_element_type=jnp.float32)
    attended = (num_diag + num_state) / (1.0 + den_diag + den_state)[..., None]
    attended = attended.astype(jnp.bfloat16).reshape(length, local_heads * size_hd)
    partial_out = jnp.dot(attended, out_weight, preferred_element_type=jnp.float32)
    mixed = lax.psum_scatter(
        partial_out.astype(jnp.bfloat16), "head", scatter_dimension=1, tiled=True
    )
    return mixed


def solution(mesh):
    in_specs = (
        P("ctx", "head"),
        P(None, None, "head"),
        P("head", None),
        P("head", None, None),
        P("head", None, None),
    )
    out_specs = P("ctx", "head")
    return jax.shard_map(shards, mesh=mesh, in_specs=in_specs, out_specs=out_specs, check_vma=False)
```

profile of v0, /device:TPU:96, one launch (start us, length us, event | category | flops | bytes accessed | tf_op | source)
XLA Modules:
  0.0 710.8 jit_solution(11091749225744624335)
XLA Ops:
  7.3 4.7 copy.17
  12.3 146.7 %all-gather.4.cloned.1.call-done = bf16[256,4096]{1,0:T(8,128)(2,1)} async-done(((bf16[256,128]{1,0:T(8,128)(2,1)}), bf16[256,4096]{1,0:T(8,128)(2,1)}) %all-gather.4.cloned.1.call-update) | async-done | bytes 2097168 | tf_op jit(solution)/shard_map/all_gather | solution.py:80
  159.0 3.5 fusion.3
  163.4 1.7 convolution_convert_fusion.1
  165.9 23.1 %all_gather.13 = bf16[16,1,4096]{2,1,0:T(2,128)(2,1)} all-gather(bf16[1,1,4096]{2,1,0:T(2,128)(2,1)S(1)} %convert_element_type.187), channel_id=1, replica_groups=mesh['ctx'=16,'head'=32] {'ctx'}, dimensions={0}, use_global_device_ids=true | all-gather | bytes 139264 | tf_op jit(solution)/shard_map/all_gather | solution.py:14
  189.2 1.5 fusion.85
  190.6 2.0 multiply_convert_fusion
  192.7 153.7 %all-gather.6.cloned.1.call-done = bf16[65536,128]{1,0:T(8,128)(2,1)} async-done(((bf16[4096,128]{1,0:T(8,128)(2,1)}), bf16[65536,128]{1,0:T(8,128)(2,1)}) %all-gather.6.cloned.1.call-update) | async-done | bytes 16777232 | tf_op jit(solution)/shard_map/all_gather | solution.py:14
  346.5 13.7 %while.12 = (s32[]{:T(128)}, f32[1,4096,128]{2,1,0:T(8,128)S(1)}, f32[1,4096]{1,0:T(1,128)S(1)}, s32[]{:T(128)}, bf16[16,1,4096,128]{3,2,1,0:T(8,128)(2,1)}, /*i...) while((s32[]{:T(128)}, f32[1,4096,128]{2,1,0:T(8,128)S(1)}, f32[1,4096]{1,0:T(1,128)S(1)}, ...), condition=%wide.region_4.0_spmd, body=%wide.region_3.0_spmd.sunk | while | flops 1056773 | bytes 5283975 | solution.py:28
  346.6 1.5 convert_add_fusion.4
  348.1 0.8 convert_add_fusion.5
  348.8 1.5 convert_add_fusion.4
  350.4 0.8 convert_add_fusion.5
  351.1 1.5 convert_add_fusion.4
  353.4 1.5 convert_add_fusion.4
  354.9 0.8 convert_add_fusion.5
  355.7 1.5 convert_add_fusion.4
  358.0 1.5 convert_add_fusion.4
  360.3 2.1 fusion.73
  362.5 1.1 fusion.18
  363.6 1.9 convolution_convert_fusion
  365.5 2.5 copy.25
  368.0 334.7 %reduce-scatter.4.cloned.1.call-done = bf16[128,256]{1,0:T(8,128)(2,1)} async-done(((bf16[4096,256]{1,0:T(8,128)(2,1)}), bf16[128,256]{1,0:T(8,128)(2,1)}) %reduce-scatter.4.cloned.1.call-update) | async-done | bytes 65552
  702.7 1.6 copy.26
  (33 shorter events, 5.4 us)
Async XLA Ops:
  6.5 357.1 %copy-start = (bf16[128,4096]{1,0:T(8,128)(2,1)S(1)}, bf16[128,4096]{1,0:T(8,128)(2,1)}, u32[]{:S(2)}) copy-start(bf16[128,4096]{1,0:T(8,128)(2,1)} %param.9) | copy-start | bytes 3145732
  6.5 152.5 %all-gather.4.cloned.1.call-start = ((), (), s32[]{:S(2)}) async-start(), calls=%async_computation.1 | async-start | bytes 2162688 | tf_op jit(solution)/shard_map/all_gather | solution.py:80
  7.3 4.8 copy-start.3
  7.3 4.8 copy-start.4
  7.3 339.1 %all-gather.6.cloned.1.call-start = ((), (), s32[]{:S(2)}) async-start(), calls=%async_computation.2 | async-start | bytes 17825792 | tf_op jit(solution)/shard_map/all_gather | solution.py:14
  165.2 537.5 %reduce-scatter.4.cloned.1.call-start = ((), (), s32[]{:S(2)}) async-start(), calls=%async_computation.3 | async-start | bytes 2162688
  360.3 2.2 copy-start.1
  362.5 1.2 copy-start.2
Sparse Core Ops, SparseCore 0:
  11.4 147.5 all-gather.3
  165.3 181.0 all-gather.5
  368.1 334.5 reduce-scatter.3
where the time goes:
time: 712 us; the launch traced here: 711 us
  waiting for transfers between devices  636 us (89%)
  blocking collectives  23.1 us (3%)
  other arithmetic  17 us (2%)
  between operations  13.2 us (2%)
  matrix products  12.4 us (2%)
  local copies, waits for them, and re-layouts  9.08 us (1%)
    unnamed x4, waiting for transfers between devices  335 us
    all_gather x1, waiting for transfers between devices, prefix(): lax.all_gather(a.astype(kind), axis)  154 us
    all_gather x1, waiting for transfers between devices, shards(): lax.all_gather(tokens, 'head', axis=1, tiled=True)  147 us
    all_gather x1, blocking collectives, prefix(): lax.all_gather(a.astype(kind), axis)  23.1 us
  transfers between devices with their start and end apart: 3, of which 3 were waited for; matrix products, arithmetic and copies ran while one was open for 1% of the time, Pallas kernels for 0%

commit v1 on v0

--- a/solution.py
+++ b/solution.py
@@ -77,7 +77,9 @@
     model_width = qkv_weight.shape[0]
     flat_weight = qkv_weight.reshape(model_width, 3 * local_heads * size_hd)
     projected = jnp.dot(
-        lax.all_gather(tokens, "head", axis=1, tiled=True),
+        jnp.concatenate(
+            lax.all_to_all(jnp.stack([tokens] * lax.axis_size("head")), "head", 0, 0), axis=1
+        ),
         flat_weight,
         preferred_element_type=jnp.float32,
     )

time: 712 us -> 687 us (0.965)
  waiting for transfers between devices: 636 us -> 585 us
  starting transfers between devices: 0.08 us -> 18 us
  local copies, waits for them, and re-layouts: 9.08 us -> 17.4 us
    all_gather x1 -> x0, waiting for transfers between devices: 147 us -> none  [shards(): lax.all_gather(tokens, 'head', axis=1, tiled=True)]
    all_to_all x0 -> x1, waiting for transfers between devices: none -> 94.6 us  [shards(): lax.all_to_all(jnp.stack([tokens] * lax.axis_size('head')), 'head', 0, 0)]
    all_to_all x0 -> x1, starting transfers between devices: none -> 17.9 us  [shards(): lax.all_to_all(jnp.stack([tokens] * lax.axis_size('head')), 'head', 0, 0)]
    unnamed x4 -> x3, waiting for transfers between devices: 335 us -> 333 us
where the time goes in v1:
time: 687 us; the launch traced here: 685 us
  waiting for transfers between devices  585 us (85%)
  blocking collectives  21.3 us (3%)
  starting transfers between devices  18 us (3%)
  local copies, waits for them, and re-layouts  17.4 us (3%)
  other arithmetic  17 us (2%)
  between operations  13.6 us (2%)
  matrix products  12.4 us (2%)
    unnamed x3, waiting for transfers between devices  333 us
    all_gather x1, waiting for transfers between devices, prefix(): lax.all_gather(a.astype(kind), axis)  158 us
    all_to_all x1, waiting for transfers between devices, shards(): lax.all_to_all(jnp.stack([tokens] * lax.axis_size('head')), 'head', 0, 0)  94.6 us
    all_gather x1, blocking collectives, prefix(): lax.all_gather(a.astype(kind), axis)  21.3 us
    all_to_all x1, starting transfers between devices, shards(): lax.all_to_all(jnp.stack([tokens] * lax.axis_size('head')), 'head', 0, 0)  17.9 us
  transfers between devices with their start and end apart: 3, of which 3 were waited for; matrix products, arithmetic and copies ran while one was open for 1% of the time, Pallas kernels for 0%

profile of v1, /device:TPU:96, one launch (start us, length us, event | category | flops | bytes accessed | tf_op | source)
XLA Modules:
  0.0 685.0 jit_solution(2869411239764129456)
XLA Ops:
  6.5 2.7 stack.2
  9.3 17.9 %all-to-all-start = ((bf16[32,256,128]{2,1,0:T(8,128)(2,1)}), bf16[32,256,128]{2,1,0:T(8,128)(2,1)S(1)}, u32[]{:S(2)}, u32[]{:S(2)}) async-start(bf16[32,256,128]{2,1,0:T(8,128)(2,1)} %stack.2), calls=%async_computation | async-start | bytes 4194304 | tf_op jit(solution)/shard_map/all_to_all | solution.py:81
  27.2 4.7 copy.18
  32.8 94.6 %all-to-all-done = bf16[32,256,128]{2,1,0:T(8,128)(2,1)S(1)} async-done(((bf16[32,256,128]{2,1,0:T(8,128)(2,1)}), bf16[32,256,128]{2,1,0:T(8,128)(2,1)S(1)}, u32[]{:S(2)}, u32[]{:S(2)}) %all-to-all-start) | async-done | bytes 2097184 | tf_op jit(solution)/shard_map/all_to_all | solution.py:81
  127.5 2.7 copy.17
  130.2 2.8 reshape.342
  133.0 2.9 fusion.2
  136.9 1.7 convolution_convert_fusion.1
  139.4 21.3 %all_gather.9 = bf16[16,1,4096]{2,1,0:T(2,128)(2,1)} all-gather(bf16[1,1,4096]{2,1,0:T(2,128)(2,1)S(1)} %convert_element_type.187), channel_id=1, replica_groups=mesh['ctx'=16,'head'=32] {'ctx'}, dimensions={0}, use_global_device_ids=true | all-gather | bytes 139264 | tf_op jit(solution)/shard_map/all_gather | solution.py:14
  160.8 1.5 fusion.82
  162.3 2.0 multiply_convert_fusion
  164.3 157.7 %all-gather.3.cloned.1.call-done = bf16[65536,128]{1,0:T(8,128)(2,1)} async-done(((bf16[4096,128]{1,0:T(8,128)(2,1)}), bf16[65536,128]{1,0:T(8,128)(2,1)}) %all-gather.3.cloned.1.call-update) | async-done | bytes 16777232 | tf_op jit(solution)/shard_map/all_gather | solution.py:14
  322.2 13.7 %while.12 = (s32[]{:T(128)}, f32[1,4096,128]{2,1,0:T(8,128)S(1)}, f32[1,4096]{1,0:T(1,128)S(1)}, s32[]{:T(128)}, bf16[16,1,4096,128]{3,2,1,0:T(8,128)(2,1)}, /*i...) while((s32[]{:T(128)}, f32[1,4096,128]{2,1,0:T(8,128)S(1)}, f32[1,4096]{1,0:T(1,128)S(1)}, ...), condition=%wide.region_4.0_spmd, body=%wide.region_3.0_spmd.sunk | while | flops 1056773 | bytes 5283975 | solution.py:28
  322.2 1.5 convert_add_fusion.4
  324.5 1.5 convert_add_fusion.4
  326.8 1.5 convert_add_fusion.4
  329.1 1.5 convert_add_fusion.4
  331.4 1.5 convert_add_fusion.4
  333.7 1.5 convert_add_fusion.4
  335.9 2.1 fusion.70
  339.3 1.9 convolution_convert_fusion
  341.2 2.5 copy.26
  343.7 332.9 %reduce-scatter.4.cloned.1.call-done = bf16[128,256]{1,0:T(8,128)(2,1)} async-done(((bf16[4096,256]{1,0:T(8,128)(2,1)}), bf16[128,256]{1,0:T(8,128)(2,1)}) %reduce-scatter.4.cloned.1.call-update) | async-done | bytes 65552
  676.6 1.6 copy.27
  (39 shorter events, 8.7 us)
Async XLA Ops:
  6.5 332.8 %copy-start = (bf16[128,4096]{1,0:T(8,128)(2,1)S(1)}, bf16[128,4096]{1,0:T(8,128)(2,1)}, u32[]{:S(2)}) copy-start(bf16[128,4096]{1,0:T(8,128)(2,1)} %param.9) | copy-start | bytes 3145732
  9.3 118.2 %all-to-all-start = ((bf16[32,256,128]{2,1,0:T(8,128)(2,1)}), bf16[32,256,128]{2,1,0:T(8,128)(2,1)S(1)}, u32[]{:S(2)}, u32[]{:S(2)}) async-start(bf16[32,256,128]{2,1,0:T(8,128)(2,1)} %stack.2), calls=%async_computation | async-start | bytes 4194304 | tf_op jit(solution)/shard_map/all_to_all | solution.py:81
  27.2 4.8 copy-start.5
  27.2 4.8 copy-start.6
  27.2 294.9 %all-gather.3.cloned.1.call-start = ((), (), s32[]{:S(2)}) async-start(), calls=%async_computation.2 | async-start | bytes 17825792 | tf_op jit(solution)/shard_map/all_gather | solution.py:14
  133.0 3.0 copy-start.2
  136.8 23.8 %copy-start.3 = (bf16[2,128,64]{1,2,0:T(8,128)(2,1)S(1)}, bf16[2,128,64]{1,2,0:T(8,128)(2,1)}, u32[]{:S(2)}) copy-start(bf16[2,128,64]{1,2,0:T(8,128)(2,1)} %fusion.11) | copy-start | bytes 98308
  138.6 538.0 %reduce-scatter.4.cloned.1.call-start = ((), (), s32[]{:S(2)}) async-start(), calls=%async_computation.3 | async-start | bytes 2162688
  335.9 2.2 copy-start.1
  338.1 1.2 copy-start.4
Sparse Core Ops, SparseCore 0:
  138.7 183.2 all-gather.2
  343.8 332.7 reduce-scatter.3
